TPU v7x, 32 devices: a whole 2x2x4 slice. The times are simulated.
32 devices in a mesh: tm: 8 (over y, x, core), chan: 4 (over z).
Axes of the slice: x: 2, y: 2, z: 4, core: 2. Of those that a mesh axis runs over, the one named last changes fastest.
Arguments:
- volts: bfloat16 [4, 16, 12288, 256], P(None, 'chan', 'tm'), may hold values from -6 to 6
- delay_peak: int32 [128, 128], P('tm', 'chan'), may hold values from 0 to 32767
- rate_peak: int32 [128, 128], P('tm', 'chan'), may hold values from 0 to 15
- station_order: int32 [128], replicated, may hold values from 0 to 127, each once
- ref_station: int32 [1], replicated, may hold values from 0 to 63
Outputs:
- fringe: float32 [128, 128, 2, 8], P('tm', 'chan')
- normal: float32 [128, 2, 256], P('tm', None, 'chan')
- rhs: float32 [128, 2], P('tm')
Inputs may be any that keep to these rules, and one draw needn't show every extreme that they name: `station_order`: each input appears once.
All inputs are finite; a program needn't handle non-finite values.
Results may differ from a plain program's by a relative error of at most 0.0003.
Values sent between devices are 32-bit elements; how exact they have to be, the bound alone decides.
A program may use at most 64 MiB of HBM per device.

v0:
```python
import math
import jax
import jax.numpy as jnp
from jax import lax
from jax.sharding import PartitionSpec as P

BAND = 16384
PERIODS_ALL = 8
WD = 4
WR = 2


def fringe_window(vis_re, vis_im, dpeak, rpeak, chans_total, periods):
    chan_local = vis_re.shape[3]
    dgrid = 2 * BAND
    rgrid = 2 * PERIODS_ALL
    dstep = BAND // chans_total
    rstep = PERIODS_ALL // periods
    chan_idx = jnp.arange(chan_local, dtype=jnp.int32)
    period_idx = jnp.arange(periods, dtype=jnp.int32)
    delays = dpeak[:, :, None] + (jnp.arange(WD, dtype=jnp.int32) - WD // 2) * dstep
    rates = rpeak[:, :, None] + (jnp.arange(WR, dtype=jnp.int32) - WR // 2) * rstep
    dphase = jnp.mod(delays[..., None] * chan_idx, dgrid).astype(jnp.float32) * (
        2.0 * math.pi / dgrid
    )
    rphase = jnp.mod(rates[..., None] * period_idx, rgrid).astype(jnp.float32) * (
        2.0 * math.pi / rgrid
    )
    angle = rphase[:, :, :, None, :, None] + dphase[:, :, None, :, None, :]
    cosine = jnp.cos(angle)
    sine = jnp.sin(angle)
    vr = vis_re[:, :, None, None]
    vi = vis_im[:, :, None, None]
    fre = jnp.sum(vr * cosine + vi * sine, axis=(4, 5))
    fim = jnp.sum(vi * cosine - vr * sine, axis=(4, 5))
    return (fre, fim)


def baseline_weights(fre, fim):
    power = fre * fre + fim * fim
    udel = (2.0 * jnp.arange(WD, dtype=jnp.float32) + 1.0 - WD) / WD
    urat = (2.0 * jnp.arange(WR, dtype=jnp.float32) + 1.0 - WR) / WR
    udel = udel[None, :]
    urat = urat[:, None]
    m_dd = jnp.mean(power * udel * udel, axis=(2, 3))
    m_dr = jnp.mean(power * udel * urat, axis=(2, 3))
    m_rr = jnp.mean(power * urat * urat, axis=(2, 3))
    g_d = jnp.mean(power * udel, axis=(2, 3))
    g_r = jnp.mean(power * urat, axis=(2, 3))
    return jnp.stack([m_dd, m_dr, m_rr, g_d, g_r])


def normal_terms(weights, row_inputs, col_inputs, inputs):
    slots = jnp.arange(inputs, dtype=jnp.int32)
    incidence = (row_inputs[:, None, None] == slots).astype(jnp.float32) - (
        col_inputs[None, :, None] == slots
    ).astype(jnp.float32)
    flat = incidence.reshape(-1, inputs)

    def block(weight):
        scaled = (incidence * weight[:, :, None]).reshape(-1, inputs)
        return jnp.dot(scaled.T, flat, precision=lax.Precision.HIGHEST) / inputs

    n_dd = block(weights[0])
    n_dr = block(weights[1])
    n_rr = block(weights[2])
    normal = jnp.concatenate(
        [jnp.concatenate([n_dd, n_dr], 1), jnp.concatenate([n_dr, n_rr], 1)], 0
    )
    rhs_d = jnp.dot(weights[3].reshape(-1), flat, precision=lax.Precision.HIGHEST) / inputs
    rhs_r = jnp.dot(weights[4].reshape(-1), flat, precision=lax.Precision.HIGHEST) / inputs
    return (normal, jnp.concatenate([rhs_d, rhs_r]))


def full_gram(volts, inputs, scale):
    prod = jnp.einsum("acti,actj->iacj", volts, volts, preferred_element_type=jnp.float32)
    real = prod[:inputs, :, :, :inputs] + prod[inputs:, :, :, inputs:]
    imag = prod[:inputs, :, :, inputs:] - prod[inputs:, :, :, :inputs]
    return jnp.stack([real, imag], axis=3) * scale


def body(volts, delay_peak, rate_peak, station_order, ref_station):
    periods, chans, samples, width = volts.shape
    inputs = width // 2
    row_count = delay_peak.shape[0]
    col_count = delay_peak.shape[1]
    time_devs = lax.axis_size("tm")
    chan_devs = lax.axis_size("chan")
    chans_total = chans * chan_devs
    scale = float(samples * time_devs) ** (-0.5)
    spread = float(periods * chans_total) ** (-0.5)
    col_inputs = lax.dynamic_slice_in_dim(
        station_order, lax.axis_index("chan") * col_count, col_count
    )
    row_inputs = lax.axis_index("tm") * row_count + jnp.arange(row_count, dtype=jnp.int32)
    gram = full_gram(volts, inputs, scale)
    summed = lax.psum_scatter(
        gram.reshape(lax.axis_size("tm") * row_count, -1), "tm", scatter_dimension=0, tiled=True
    )
    vis = summed.reshape(row_count, periods, chans, 2, inputs)
    grouped = jnp.take(vis, station_order, axis=4)
    moved = lax.all_to_all(grouped, "chan", split_axis=4, concat_axis=2, tiled=True)
    vis_re = jnp.transpose(moved[:, :, :, 0], (0, 3, 1, 2))
    vis_im = jnp.transpose(moved[:, :, :, 1], (0, 3, 1, 2))
    fre, fim = fringe_window(vis_re, vis_im, delay_peak, rate_peak, chans_total, periods)
    auto = (row_inputs[:, None] == col_inputs[None, :])[:, :, None, None]
    fre = jnp.where(auto, 0.0, fre * spread)
    fim = jnp.where(auto, 0.0, fim * spread)
    fringe = jnp.stack([fre, fim], axis=2).reshape(row_count, col_count, 2, WR * WD)
    weights = baseline_weights(fre, fim)
    col_width = 2 * inputs // chan_devs
    normal_part, rhs_part = normal_terms(weights, row_inputs, col_inputs, inputs)
    arranged = jnp.transpose(normal_part.reshape(2, inputs, 2 * inputs), (1, 0, 2))
    arranged = arranged.reshape(time_devs, row_count, 2, chan_devs, col_width)
    arranged = jnp.transpose(arranged, (0, 3, 1, 2, 4)).reshape(
        time_devs * chan_devs * row_count, 2, col_width
    )
    normal_rows = lax.psum_scatter(arranged, ("tm", "chan"), scatter_dimension=0, tiled=True)
    rhs_all = lax.psum(jnp.transpose(rhs_part.reshape(2, inputs), (1, 0)), ("tm", "chan"))
    rhs_rows = lax.dynamic_slice_in_dim(rhs_all, lax.axis_index("tm") * row_count, row_count, 0)
    columns = lax.axis_index("chan") * col_width + jnp.arange(col_width, dtype=jnp.int32)
    params = jnp.arange(2, dtype=jnp.int32)[None, :] * inputs + row_inputs[:, None]
    row_ref = row_inputs // 2 == ref_station[0]
    col_ref = columns % inputs // 2 == ref_station[0]
    ident = (params[:, :, None] == columns[None, None, :]).astype(jnp.float32)
    normal_rows = jnp.where(row_ref[:, None, None] | col_ref[None, None, :], ident, normal_rows)
    rhs_rows = jnp.where(row_ref[:, None], 0.0, rhs_rows)
    return (fringe, normal_rows, rhs_rows)


def solution(mesh):
    in_specs = (P(None, "chan", "tm", None), P("tm", "chan"), P("tm", "chan"), P(), P())
    out_specs = (P("tm", "chan", None, None), P("tm", None, "chan"), P("tm", None))
    return jax.shard_map(body, mesh=mesh, in_specs=in_specs, out_specs=out_specs, check_vma=False)
```

profile of v0, /device:TPU:0, one launch (start us, length us, event | category | flops | bytes accessed | tf_op | source)
XLA Modules:
  0.0 298.8 jit_solution(5013165204191400454)
XLA Ops:
  7.2 0.0 reduce-scatter.7.cloned.1.call-start
  7.2 11.0 %convolution_bitcast_fusion = f32[256,4,4,256]{0,3,2,1:T(8,128)S(1)} fusion(bf16[4,4,1536,256]{3,2,1,0:T(8,128)(2,1)} %param.5), kind=kOutput, calls=%fused_computation.11 | convolution fusion | flops 3221225472 | bytes 16777216 | tf_op jit(solution)/shard_map/acti,actj->iacj/dot_general | solution.py:76
  18.2 0.2 fusion.19
  18.5 0.3 maximum_multiply_fusion
  18.7 0.2 copy.39
  19.0 1.9 copy.56
  21.5 0.1 dynamic_slice.6
  21.7 0.1 broadcast_add_fusion.2
  21.8 0.1 broadcast_compare_fusion
  21.9 0.1 broadcast_or_fusion
  21.9 0.1 fusion.43
  22.0 0.1 fusion.42
  22.1 0.1 broadcast_add_fusion.1
  22.2 0.1 broadcast_add_fusion
  22.2 0.1 fusion.41
  22.3 42.6 %reduce-scatter.7.cloned.1.call-done = f32[16,4096]{1,0:T(8,128)} async-done(((f32[128,4096]{1,0:T(8,128)}), f32[16,4096]{1,0:T(8,128)}) %reduce-scatter.7.cloned.1.call-update) | async-done | bytes 262160
  64.9 1.5 copy.57
  66.5 2.7 copy.41
  69.2 4.9 %gather_fusion = f32[128,16,4,4,2]{1,3,4,2,0:T(4,128)} fusion(f32[16,4,4,2,128]{0,2,4,3,1:T(4,128)} %copy.41, s32[1024]{0:T(1024)S(1)} %pad_clamp_fusion), kind=kCustom, calls=%fused_computation | custom fusion | bytes 524800 | tf_op jit(solution)/shard_map/jit(_take)/gather | solution.py:101
  74.1 2.1 fusion.47
  76.2 2.3 reshape.374
  78.5 4.6 %all-to-all-start = ((f32[4,1,16384]{2,1,0:T(1,128)}), f32[4,1,16384]{2,1,0:T(1,128)S(1)}, u32[]{:S(2)}, u32[]{:S(2)}) async-start(f32[4,1,16384]{2,1,0:T(1,128)} %reshape.374), calls=%async_computation | async-start | bytes 524288 | tf_op jit(solution)/shard_map/all_to_all | solution.py:102
  83.1 1.0 fusion.22
  84.2 7.9 %all-to-all-done = f32[4,1,16384]{2,1,0:T(1,128)S(1)} async-done(((f32[4,1,16384]{2,1,0:T(1,128)}), f32[4,1,16384]{2,1,0:T(1,128)S(1)}, u32[]{:S(2)}, u32[]{:S(2)}) %all-to-all-start) | async-done | bytes 262176 | tf_op jit(solution)/shard_map/all_to_all | solution.py:102
  92.0 0.5 broadcast.559
  92.5 1.4 reduce
  93.9 1.5 reshape.375
  95.4 1.0 copy.42
  96.4 0.1 slice_bitcast_fusion.1
  96.5 0.2 copy.43
  96.7 0.2 copy.44
  96.9 0.6 copy-done
  97.4 16.5 %fusion.5 = (f32[16,32,2,4]{1,3,2,0:T(4,128)S(1)}, f32[16,32,2,4]{1,3,2,0:T(4,128)S(1)}) fusion(f32[16,32,4,16]{1,3,2,0:T(8,128)S(1)} %copy.44, f32[16,32,4,16]{1,3,2,0:T(8,128)S(1)} %copy-done, f32[16,32,2,4]{1,3,2,0:T(4,128)S(1)} %fusion.41, f32[16,32,4,16]{1,3,2,0:T(8,128)S(1)} %copy.43), kind=kLoop, calls=%fused_computation.8 | loop fusion | flops 2351104 | bytes 442368 | tf_op jit(solution)/shard_map/reduce_sum | solution.py:34
  114.0 0.2 multiply_reduce_fusion.4
  114.2 0.3 fusion.12
  114.5 0.3 fusion.11
  114.8 37.9 %psum.7 = f32[128,2]{0,1:T(2,128)S(1)} all-reduce(f32[128,2]{0,1:T(2,128)S(1)} %maximum_bitcast_fusion), channel_id=1, replica_groups=mesh['tm'=8,'chan'=4] {'tm','chan'}, use_global_device_ids=true, to_apply=%region_9.10 | all-reduce | flops 256 | bytes 2048 | tf_op jit(solution)/shard_map/psum | solution.py:119
  152.7 0.7 fusion.9
  153.4 0.7 fusion.8
  154.1 0.7 fusion.10
  154.8 0.1 copy.55
  154.9 0.2 reshape.353
  155.2 0.8 copy.48
  156.0 0.7 pad_maximum_fusion
  156.7 0.6 dynamic-slice_select_fusion
  157.3 133.2 %reduce-scatter.5.cloned.1.call-done = f32[16,2,64]{2,0,1:T(8,128)} async-done(((f32[512,2,64]{2,0,1:T(8,128)}), f32[16,2,64]{2,0,1:T(8,128)}) %reduce-scatter.5.cloned.1.call-update) | async-done | bytes 8208 | tf_op jit(solution)/shard_map/reduce_scatter | solution.py:118
  290.6 0.8 convert_select_fusion
  291.4 0.6 copy.49
  (29 shorter events, 0.3 us)
Async XLA Ops:
  7.2 57.8 %reduce-scatter.7.cloned.1.call-start = ((), (), s32[]{:S(2)}) async-start(), calls=%async_computation.4 | async-start | bytes 2359296
  19.0 2.6 copy-start.3
  19.0 3.1 %copy-start.1 = (s32[16,32]{1,0:T(8,128)S(1)}, s32[16,32]{1,0:T(8,128)}, u32[]{:S(2)}) copy-start(s32[16,32]{1,0:T(8,128)} %param.7) | copy-start | bytes 6148
  19.0 3.2 %copy-start.2 = (s32[16,32]{1,0:T(8,128)S(1)}, s32[16,32]{1,0:T(8,128)}, u32[]{:S(2)}) copy-start(s32[16,32]{1,0:T(8,128)} %param.6) | copy-start | bytes 6148
  78.5 13.5 %all-to-all-start = ((f32[4,1,16384]{2,1,0:T(1,128)}), f32[4,1,16384]{2,1,0:T(1,128)S(1)}, u32[]{:S(2)}, u32[]{:S(2)}) async-start(f32[4,1,16384]{2,1,0:T(1,128)} %reshape.374), calls=%async_computation | async-start | bytes 524288 | tf_op jit(solution)/shard_map/all_to_all | solution.py:102
  83.1 207.5 %reduce-scatter.5.cloned.1.call-start = ((), (), s32[]{:S(2)}) async-start(), calls=%async_computation.3 | async-start | bytes 540672 | tf_op jit(solution)/shard_map/reduce_scatter | solution.py:118
  96.4 1.0 copy-start
Sparse Core Ops, SparseCore 0:
  21.0 43.8 reduce-scatter.6
  156.1 134.3 reduce-scatter.4
where the time goes:
time: 299 us
  waiting for transfers between devices  184 us (62%)
  blocking collectives  37.9 us (13%)
  other arithmetic  24.6 us (8%)
  local copies, waits for them, and re-layouts  19.4 us (6%)
  between operations  15 us (5%)
  matrix products  13.6 us (5%)
  starting transfers between devices  4.65 us (2%)
    reduce_scatter x1, waiting for transfers between devices, body(): lax.psum_scatter(arranged, ('tm', 'chan'), scatter_dimension=0, tiled=True)  133 us
    unnamed x3, waiting for transfers between devices  42.6 us
    psum x1, blocking collectives, body(): lax.psum(jnp.transpose(rhs_part.reshape(2, inputs), (1, 0)), ('tm', 'chan'))  37.9 us
    reduce_sum x1, other arithmetic, fringe_window(): fre = jnp.sum(vr * cosine + vi * sine, axis=(4, 5))  16.5 us
    dot_general x1, matrix products, full_gram(): jnp.einsum('acti,actj->iacj', volts, volts, preferred_element_type=jnp.fl...  11 us
    unnamed x13, local copies, waits for them, and re-layouts  8.36 us
    all_to_all x1, waiting for transfers between devices, body(): lax.all_to_all(grouped, 'chan', split_axis=4, concat_axis=2, tiled=True)  7.86 us
  transfers between devices with their start and end apart: 3, of which 3 were waited for; matrix products, arithmetic and copies ran while one was open for 1% of the time, Pallas kernels for 0%

commit v1 on v0

--- a/solution.py
+++ b/solution.py
@@ -116,7 +116,7 @@
         time_devs * chan_devs * row_count, 2, col_width
     )
     normal_rows = lax.psum_scatter(arranged, ("tm", "chan"), scatter_dimension=0, tiled=True)
-    rhs_all = lax.psum(jnp.transpose(rhs_part.reshape(2, inputs), (1, 0)), ("tm", "chan"))
+    rhs_all = lax.psum(lax.psum(jnp.transpose(rhs_part.reshape(2, inputs), (1, 0)), "chan"), "tm")
     rhs_rows = lax.dynamic_slice_in_dim(rhs_all, lax.axis_index("tm") * row_count, row_count, 0)
     columns = lax.axis_index("chan") * col_width + jnp.arange(col_width, dtype=jnp.int32)
     params = jnp.arange(2, dtype=jnp.int32)[None, :] * inputs + row_inputs[:, None]

time: 299 us -> 280 us (0.936)
  blocking collectives: 37.9 us -> 21.6 us
  waiting for transfers between devices: 184 us -> 181 us
    psum x1 -> x2, blocking collectives: 37.9 us -> 21.6 us  [the longest x1 11.8 us: body(): lax.psum(lax.psum(jnp.transpose(rhs_part.reshape(2, inputs), (1, 0)), 'ch...]
    reduce_scatter x1, waiting for transfers between devices: 133 us -> 130 us  [body(): lax.psum_scatter(arranged, ('tm', 'chan'), scatter_dimension=0, tiled=True)]
where the time goes in v1:
time: 280 us; the launch traced here: 279 us
  waiting for transfers between devices  181 us (65%)
  other arithmetic  24.6 us (9%)
  blocking collectives  21.6 us (8%)
  local copies, waits for them, and re-layouts  19.4 us (7%)
  between operations  15 us (5%)
  matrix products  13.6 us (5%)
  starting transfers between devices  4.65 us (2%)
    reduce_scatter x1, waiting for transfers between devices, body(): lax.psum_scatter(arranged, ('tm', 'chan'), scatter_dimension=0, tiled=True)  130 us
    unnamed x3, waiting for transfers between devices  42.6 us
    reduce_sum x1, other arithmetic, fringe_window(): fre = jnp.sum(vr * cosine + vi * sine, axis=(4, 5))  16.5 us
    psum x1, blocking collectives, body(): lax.psum(lax.psum(jnp.transpose(rhs_part.reshape(2, inputs), (1, 0)), 'ch...  11.8 us
    dot_general x1, matrix products, full_gram(): jnp.einsum('acti,actj->iacj', volts, volts, preferred_element_type=jnp.fl...  11 us
    psum x1, blocking collectives, body(): lax.psum(jnp.transpose(rhs_part.reshape(2, inputs), (1, 0)), 'chan')  9.78 us
    unnamed x13, local copies, waits for them, and re-layouts  8.36 us
    all_to_all x1, waiting for transfers between devices, body(): lax.all_to_all(grouped, 'chan', split_axis=4, concat_axis=2, tiled=True)  7.86 us
  transfers between devices with their start and end apart: 3, of which 3 were waited for; matrix products, arithmetic and copies ran while one was open for 1% of the time, Pallas kernels for 0%

profile of v1, /device:TPU:0, one launch (start us, length us, event | category | flops | bytes accessed | tf_op | source)
XLA Modules:
  0.0 279.4 jit_solution(9168451399878245506)
XLA Ops:
  7.2 11.0 %convolution_bitcast_fusion = f32[256,4,4,256]{0,3,2,1:T(8,128)S(1)} fusion(bf16[4,4,1536,256]{3,2,1,0:T(8,128)(2,1)} %param.5), kind=kOutput, calls=%fused_computation.11 | convolution fusion | flops 3221225472 | bytes 16777216 | tf_op jit(solution)/shard_map/acti,actj->iacj/dot_general | solution.py:76
  18.2 0.2 fusion.19
  18.5 0.3 maximum_multiply_fusion
  18.7 0.2 copy.39
  19.0 1.9 copy.56
  21.5 0.1 dynamic_slice.6
  21.7 0.1 broadcast_add_fusion.2
  21.8 0.1 broadcast_compare_fusion
  21.9 0.1 broadcast_or_fusion
  21.9 0.1 fusion.43
  22.0 0.1 fusion.42
  22.1 0.1 broadcast_add_fusion.1
  22.2 0.1 broadcast_add_fusion
  22.2 0.1 fusion.41
  22.3 42.6 %reduce-scatter.7.cloned.1.call-done = f32[16,4096]{1,0:T(8,128)} async-done(((f32[128,4096]{1,0:T(8,128)}), f32[16,4096]{1,0:T(8,128)}) %reduce-scatter.7.cloned.1.call-update) | async-done | bytes 262160
  64.9 1.5 copy.57
  66.5 2.7 copy.41
  69.2 4.9 %gather_fusion = f32[128,16,4,4,2]{1,3,4,2,0:T(4,128)} fusion(f32[16,4,4,2,128]{0,2,4,3,1:T(4,128)} %copy.41, s32[1024]{0:T(1024)S(1)} %pad_clamp_fusion), kind=kCustom, calls=%fused_computation | custom fusion | bytes 524800 | tf_op jit(solution)/shard_map/jit(_take)/gather | solution.py:101
  74.1 2.1 fusion.47
  76.2 2.3 reshape.374
  78.5 4.6 %all-to-all-start = ((f32[4,1,16384]{2,1,0:T(1,128)}), f32[4,1,16384]{2,1,0:T(1,128)S(1)}, u32[]{:S(2)}, u32[]{:S(2)}) async-start(f32[4,1,16384]{2,1,0:T(1,128)} %reshape.374), calls=%async_computation | async-start | bytes 524288 | tf_op jit(solution)/shard_map/all_to_all | solution.py:102
  83.1 1.0 fusion.22
  84.2 7.9 %all-to-all-done = f32[4,1,16384]{2,1,0:T(1,128)S(1)} async-done(((f32[4,1,16384]{2,1,0:T(1,128)}), f32[4,1,16384]{2,1,0:T(1,128)S(1)}, u32[]{:S(2)}, u32[]{:S(2)}) %all-to-all-start) | async-done | bytes 262176 | tf_op jit(solution)/shard_map/all_to_all | solution.py:102
  92.0 0.5 broadcast.559
  92.5 1.4 reduce
  93.9 1.5 reshape.375
  95.4 1.0 copy.42
  96.4 0.1 slice_bitcast_fusion.1
  96.5 0.2 copy.43
  96.7 0.2 copy.44
  96.9 0.6 copy-done
  97.4 16.5 %fusion.5 = (f32[16,32,2,4]{1,3,2,0:T(4,128)S(1)}, f32[16,32,2,4]{1,3,2,0:T(4,128)S(1)}) fusion(f32[16,32,4,16]{1,3,2,0:T(8,128)S(1)} %copy.44, f32[16,32,4,16]{1,3,2,0:T(8,128)S(1)} %copy-done, f32[16,32,2,4]{1,3,2,0:T(4,128)S(1)} %fusion.41, f32[16,32,4,16]{1,3,2,0:T(8,128)S(1)} %copy.43), kind=kLoop, calls=%fused_computation.8 | loop fusion | flops 2351104 | bytes 442368 | tf_op jit(solution)/shard_map/reduce_sum | solution.py:34
  114.0 0.2 multiply_reduce_fusion.4
  114.2 0.3 fusion.12
  114.5 0.3 fusion.11
  114.8 9.8 %psum.14 = f32[128,2]{0,1:T(2,128)S(1)} all-reduce(f32[128,2]{0,1:T(2,128)S(1)} %maximum_bitcast_fusion), channel_id=1, replica_groups=mesh['tm'=8,'chan'=4] {'chan'}, use_global_device_ids=true, to_apply=%region_9.10 | all-reduce | flops 256 | bytes 2048 | tf_op jit(solution)/shard_map/psum | solution.py:119
  124.6 11.8 %psum.15 = f32[128,2]{0,1:T(2,128)S(1)} all-reduce(f32[128,2]{0,1:T(2,128)S(1)} %psum.14), channel_id=1, replica_groups=mesh['tm'=8,'chan'=4] {'tm'}, use_global_device_ids=true, to_apply=%region_10.11 | all-reduce | flops 256 | bytes 2048 | tf_op jit(solution)/shard_map/psum | solution.py:119
  136.4 0.7 fusion.9
  137.0 0.7 fusion.8
  137.7 0.7 fusion.10
  138.5 0.1 copy.55
  138.6 0.2 reshape.353
  138.8 0.8 copy.48
  139.7 0.7 pad_maximum_fusion
  140.4 0.6 dynamic-slice_select_fusion
  141.0 130.2 %reduce-scatter.5.cloned.1.call-done = f32[16,2,64]{2,0,1:T(8,128)} async-done(((f32[512,2,64]{2,0,1:T(8,128)}), f32[16,2,64]{2,0,1:T(8,128)}) %reduce-scatter.5.cloned.1.call-update) | async-done | bytes 8208 | tf_op jit(solution)/shard_map/reduce_scatter | solution.py:118
  271.2 0.8 convert_select_fusion
  272.0 0.6 copy.49
  (30 shorter events, 0.3 us)
Async XLA Ops:
  7.2 57.8 %reduce-scatter.7.cloned.1.call-start = ((), (), s32[]{:S(2)}) async-start(), calls=%async_computation.4 | async-start | bytes 2359296
  19.0 2.6 copy-start.3
  19.0 3.1 %copy-start.1 = (s32[16,32]{1,0:T(8,128)S(1)}, s32[16,32]{1,0:T(8,128)}, u32[]{:S(2)}) copy-start(s32[16,32]{1,0:T(8,128)} %param.7) | copy-start | bytes 6148
  19.0 3.2 %copy-start.2 = (s32[16,32]{1,0:T(8,128)S(1)}, s32[16,32]{1,0:T(8,128)}, u32[]{:S(2)}) copy-start(s32[16,32]{1,0:T(8,128)} %param.6) | copy-start | bytes 6148
  78.5 13.5 %all-to-all-start = ((f32[4,1,16384]{2,1,0:T(1,128)}), f32[4,1,16384]{2,1,0:T(1,128)S(1)}, u32[]{:S(2)}, u32[]{:S(2)}) async-start(f32[4,1,16384]{2,1,0:T(1,128)} %reshape.374), calls=%async_computation | async-start | bytes 524288 | tf_op jit(solution)/shard_map/all_to_all | solution.py:102
  83.1 188.1 %reduce-scatter.5.cloned.1.call-start = ((), (), s32[]{:S(2)}) async-start(), calls=%async_computation.3 | async-start | bytes 540672 | tf_op jit(solution)/shard_map/reduce_scatter | solution.py:118
  96.4 1.0 copy-start
Sparse Core Ops, SparseCore 0:
  21.0 43.8 reduce-scatter.6
  139.8 131.3 reduce-scatter.4
